TPU v7x, 32 devices: a whole 2x2x4 slice. The times are simulated.
32 devices in a mesh: member: 8 (over y, x, core), region: 4 (over z).
Axes of the slice: x: 2, y: 2, z: 4, core: 2. Of those that a mesh axis runs over, the one named last changes fastest.
Arguments:
- state: bfloat16 [16, 64, 4096], P('member', 'region'), may hold values from -6 to 6
- diffusivity: float32 [64, 4096], P('region'), may hold values from 0.05 to 0.45
- model_perturbation: bfloat16 [2, 16, 64, 4096], P(None, 'member', 'region'), may hold values from -3 to 3
- obs_values: float32 [2, 128, 16], P(None, 'region'), may hold values from -14 to 14
- obs_prec: float32 [128, 16], P('region'), may hold values from 0.5 to 2
- obs_tile: int32 [128], P('region'), may hold values from 0 to 15
- obs_cell: int32 [128, 16], P('region'), may hold values from 0 to 4095
- pattern: int32 [64, 6], P('region'), may hold values from 0 to 31
- loc_weight: float32 [64, 6], P('region'), may hold values from 0.02 to 0.2
- anc_member: int32 [2, 4, 16, 16, 1], P(None, 'region', 'member'), may hold values from 0 to 7; in each aligned block of 32 rows (0 to 31, 32 to 63, ..., all dimensions but the last counted through in order) at most 8 rows name the same one
- anc_slot: int32 [2, 4, 16, 16], P(None, 'region', 'member'), may hold values from 0 to 1
Outputs:
- analysis: bfloat16 [16, 64, 4096], P('member', 'region')
- analysis_mean: float32 [2, 64, 4096], P(None, 'region', 'member')
Inputs may be any that keep to these rules, and one draw needn't show every extreme that they name: `anc_member`: within one cycle, among the 32 particle tiles of one device (one member index, one region), at most 8 ancestors lie on the same member index.
All inputs are finite; a program needn't handle non-finite values.
Results may differ from a plain program's by a relative error of at most 0.0046.
Values may be sent and summed in bfloat16 or wider, within the bound.
No kernel may reach another device: no remote copies, remote signals or barrier semaphores. Data moves between devices by JAX's collectives and lax.ppermute only.
A program may use at most 64 MiB of HBM per device.

v0:
```python
import jax
import jax.numpy as jnp
from jax import lax
from jax.sharding import PartitionSpec as P

CYCLES = 2
STEPS = 2


def extended(array, sides, width):
    for axis, dim in sides:
        peers, length = (lax.axis_size(axis), array.shape[dim])
        up = [(i, (i + 1) % peers) for i in range(peers - 1)]
        down = [(j, i) for i, j in up]
        last = lax.slice_in_dim(array, length - width, length, axis=dim)
        initial = lax.slice_in_dim(array, 0, width, axis=dim)
        before = lax.ppermute(last, axis, up)
        after = lax.ppermute(initial, axis, down)
        array = jnp.concatenate([before, array, after], axis=dim)
    return array


def body(
    state,
    diffusivity,
    model_perturbation,
    obs_values,
    obs_prec,
    obs_tile,
    obs_cell,
    pattern,
    loc_weight,
    anc_member,
    anc_slot,
):
    part_dev, tiles_dev, patch_extent = state.shape
    members = lax.axis_size("member")
    capacity = max(2, 2 * part_dev * tiles_dev // members)
    area_members = part_dev * tiles_dev
    strip_extent = tiles_dev * patch_extent
    smoothed_strip = diffusivity.reshape(1, strip_extent)
    measured_position = obs_tile[:, None] * patch_extent + obs_cell
    blocks = obs_tile.shape[0]
    loc_matrix = jnp.sum(
        jnp.where(
            pattern[:, :, None] == jnp.arange(blocks, dtype=jnp.int32)[None, None, :],
            loc_weight[:, :, None],
            0.0,
        ),
        axis=1,
    )
    row_ids = jnp.arange(area_members, dtype=jnp.int32)
    tile_of_row = row_ids % tiles_dev
    earlier = row_ids[None, :] < row_ids[:, None]
    current = state
    mean_list = []
    for update_ordinal in range(CYCLES):
        moved = current.reshape(part_dev, strip_extent).astype(jnp.float32)
        for repeat in range(STEPS):
            padded = extended(moved, (("region", 1),), 1)
            moved = moved + smoothed_strip * (padded[:, :-2] - 2.0 * moved + padded[:, 2:])
        prior_ensemble = (
            moved
            + model_perturbation[update_ordinal].reshape(part_dev, strip_extent).astype(jnp.float32)
        ).astype(jnp.bfloat16)
        modelled_readings = prior_ensemble[:, measured_position].astype(jnp.float32)
        misses = obs_values[update_ordinal] - modelled_readings
        misfit = 0.5 * jnp.sum(obs_prec * misses * misses, axis=-1)
        loglik = jnp.dot(misfit, loc_matrix.T, precision=lax.Precision.HIGHEST)
        all_scores = lax.all_gather(loglik, "member", axis=0, tiled=True)
        lowest = jnp.min(all_scores, axis=0)
        totals = jnp.sum(jnp.exp(lowest - all_scores), axis=0)
        unscaled = jnp.exp(lowest - loglik)
        patch_member_slab = prior_ensemble.reshape(area_members, patch_extent)
        weighted = jnp.sum(
            unscaled[:, :, None]
            * patch_member_slab.reshape(part_dev, tiles_dev, patch_extent).astype(jnp.float32),
            axis=0,
        )
        portion = lax.psum_scatter(weighted, "member", scatter_dimension=1, tiled=True)
        mean_list.append(portion / totals[:, None])
        source = anc_member[update_ordinal, 0, :, :, 0].reshape(area_members)
        codes = anc_slot[update_ordinal, 0].reshape(area_members) * tiles_dev + tile_of_row
        ranks = jnp.sum((source[None, :] == source[:, None]) & earlier, axis=1)
        wanted = jnp.full((members, capacity), -1, jnp.int32).at[source, ranks].set(codes)
        fetched = patch_member_slab[
            jnp.maximum(
                lax.all_to_all(wanted, "member", split_axis=0, concat_axis=0, tiled=True), 0
            )
        ]
        arrived = lax.all_to_all(fetched, "member", split_axis=0, concat_axis=0, tiled=True)
        current = arrived[source, ranks].reshape(part_dev, tiles_dev, patch_extent)
    return (current, jnp.stack(mean_list))


def solution(mesh):
    in_specs = (
        P("member", "region", None),
        P("region", None),
        P(None, "member", "region", None),
        P(None, "region", None),
        P("region", None),
        P("region"),
        P("region", None),
        P("region", None),
        P("region", None),
        P(None, "region", "member", None, None),
        P(None, "region", "member", None),
    )
    out_specs = (P("member", "region", None), P(None, "region", "member"))
    return jax.shard_map(body, mesh=mesh, in_specs=in_specs, out_specs=out_specs, check_vma=False)
```

profile of v0, /device:TPU:0, one launch (start us, length us, event | category | flops | bytes accessed | tf_op | source)
XLA Modules:
  0.0 214.6 jit_solution(13415304741372341621)
XLA Ops:
  8.7 4.9 %collective-permute-start = (f32[2,1]{1,0:T(2,128)S(1)}, f32[2,1]{1,0:T(2,128)S(1)}, u32[]{:S(2)}, u32[]{:S(2)}) collective-permute-start(f32[2,1]{1,0:T(2,128)S(1)} %get-tuple-element.16), channel_id=1, source_target_pairs={{0,1},{1,2},{2,3},{4,5},{5,6},{6,7},{8,9},{9,10},{10,11},{12,13},{... | collective-permute-start | bytes 32 | tf_op jit(solution)/shard_map/ppermute | solution.py:17
  17.4 5.4 %scatter_fusion = s32[8,8]{1,0:T(8,128)} fusion(s32[8,8]{1,0:T(8,128)} %broadcast.129.clone.1, s32[32]{0:T(128)S(1)} %get-tuple-element.8, s32[32]{0:T(128)S(1)} %fusion.37), kind=kCustom, calls=%fused_computation.6 | custom fusion | bytes 640 | tf_op jit(solution)/shard_map/scatter | solution.py:85
  22.8 3.7 %all-to-all-start = ((s32[8,1,8]{2,1,0:T(1,128)}), s32[8,1,8]{2,1,0:T(1,128)S(1)}, u32[]{:S(2)}, u32[]{:S(2)}) async-start(s32[8,1,8]{2,1,0:T(1,128)} %bitcast.3), calls=%async_computation | async-start | bytes 8192 | tf_op jit(solution)/shard_map/all_to_all | solution.py:88
  32.0 5.4 %scatter_fusion.1 = s32[8,8]{1,0:T(8,128)} fusion(s32[8,8]{1,0:T(8,128)} %broadcast.129.clone, s32[32]{0:T(128)S(1)} %get-tuple-element.6, s32[32]{0:T(128)S(1)} %fusion.36), kind=kCustom, calls=%fused_computation.7 | custom fusion | bytes 640 | tf_op jit(solution)/shard_map/scatter | solution.py:85
  38.6 4.5 %collective-permute-start.2 = (f32[2,1]{1,0:T(2,128)S(1)}, f32[2,1]{1,0:T(2,128)S(1)}, u32[]{:S(2)}, u32[]{:S(2)}) collective-permute-start(f32[2,1]{1,0:T(2,128)S(1)} %get-tuple-element.14), channel_id=1, source_target_pairs={{0,1},{1,2},{2,3},{4,5},{5,6},{6,7},{8,9},{9,10},{10,11},{12,13},{... | collective-permute-start | bytes 32 | tf_op jit(solution)/shard_map/ppermute | solution.py:17
  44.5 4.2 %all-to-all-start.2 = ((s32[8,1,8]{2,1,0:T(1,128)}), s32[8,1,8]{2,1,0:T(1,128)S(1)}, u32[]{:S(2)}, u32[]{:S(2)}) async-start(s32[8,1,8]{2,1,0:T(1,128)} %bitcast.9), calls=%async_computation.2 | async-start | bytes 8192 | tf_op jit(solution)/shard_map/all_to_all | solution.py:88
  50.1 3.2 %all-to-all-done.2 = s32[8,1,8]{2,1,0:T(1,128)S(1)} async-done(((s32[8,1,8]{2,1,0:T(1,128)}), s32[8,1,8]{2,1,0:T(1,128)S(1)}, u32[]{:S(2)}, u32[]{:S(2)}) %all-to-all-start.2) | async-done | bytes 288 | tf_op jit(solution)/shard_map/all_to_all | solution.py:88
  53.4 1.7 gather_fusion
  55.0 3.5 %all-to-all-start.1 = ((bf16[8,8,4096]{2,1,0:T(8,128)(2,1)}), bf16[8,8,4096]{2,1,0:T(8,128)(2,1)S(1)}, u32[]{:S(2)}, u32[]{:S(2)}) async-start(bf16[8,8,4096]{2,1,0:T(8,128)(2,1)} %bitcast.4), calls=%async_computation.1 | async-start | bytes 1048576 | tf_op jit(solution)/shard_map/all_to_all | solution.py:91
  59.0 10.7 %copy.139 = bf16[2,65536]{0,1:T(8,128)(2,1)} copy(bf16[2,65536]{1,0:T(2,128)(2,1)S(1)} %fusion.18) | data formatting | bytes 524288 | tf_op jit(solution)/shard_map/convert_element_type | solution.py:65
  69.6 9.0 %gather_fusion.4 = bf16[512,2]{1,0:T(8,128)(2,1)S(1)} fusion(bf16[2,65536]{0,1:T(8,128)(2,1)} %copy.139, s32[1024]{0:T(1024)S(1)} %pad_clamp_fusion), kind=kCustom, calls=%fused_computation.4 | custom fusion | bytes 6144 | tf_op jit(solution)/shard_map/gather | solution.py:66
  80.7 4.5 %collective-permute-start.4 = (f32[2,1]{1,0:T(2,128)S(1)}, f32[2,1]{1,0:T(2,128)S(1)}, u32[]{:S(2)}, u32[]{:S(2)}) collective-permute-start(f32[2,1]{1,0:T(2,128)S(1)} %get-tuple-element.12), channel_id=1, source_target_pairs={{0,1},{1,2},{2,3},{4,5},{5,6},{6,7},{8,9},{9,10},{10,11},{12,13},{... | collective-permute-start | bytes 32 | tf_op jit(solution)/shard_map/ppermute | solution.py:17
  86.7 4.0 %collective-permute-done.5 = f32[2,1]{1,0:T(2,128)S(1)} collective-permute-done((f32[2,1]{1,0:T(2,128)S(1)}, f32[2,1]{1,0:T(2,128)S(1)}, u32[]{:S(2)}, u32[]{:S(2)}) %collective-permute-start.5) | collective-permute-done | bytes 40 | tf_op jit(solution)/shard_map/ppermute | solution.py:18
  91.9 3.5 %collective-permute-start.6 = (f32[2,1]{1,0:T(2,128)S(1)}, f32[2,1]{1,0:T(2,128)S(1)}, u32[]{:S(2)}, u32[]{:S(2)}) collective-permute-start(f32[2,1]{1,0:T(2,128)S(1)} %get-tuple-element.10), channel_id=1, source_target_pairs={{0,1},{1,2},{2,3},{4,5},{5,6},{6,7},{8,9},{9,10},{10,11},{12,13},{... | collective-permute-start | bytes 32 | tf_op jit(solution)/shard_map/ppermute | solution.py:17
  96.7 4.2 %collective-permute-done.7 = f32[2,1]{1,0:T(2,128)S(1)} collective-permute-done((f32[2,1]{1,0:T(2,128)S(1)}, f32[2,1]{1,0:T(2,128)S(1)}, u32[]{:S(2)}, u32[]{:S(2)}) %collective-permute-start.7) | collective-permute-done | bytes 40 | tf_op jit(solution)/shard_map/ppermute | solution.py:18
  102.1 10.7 %copy.141 = bf16[2,65536]{0,1:T(8,128)(2,1)} copy(bf16[2,65536]{1,0:T(2,128)(2,1)S(1)} %fusion.19) | data formatting | bytes 524288 | tf_op jit(solution)/shard_map/convert_element_type | solution.py:65
  112.7 9.0 %gather_fusion.5 = bf16[512,2]{1,0:T(8,128)(2,1)S(1)} fusion(bf16[2,65536]{0,1:T(8,128)(2,1)} %copy.141, s32[1024]{0:T(1024)S(1)} %pad_clamp_fusion), kind=kCustom, calls=%fused_computation.5 | custom fusion | bytes 6144 | tf_op jit(solution)/shard_map/gather | solution.py:66
  122.2 9.3 %all-gather = f32[8,2,16]{2,1,0:T(2,128)S(1)} all-gather(f32[1,2,16]{2,1,0:T(2,128)S(1)} %bitcast.95), channel_id=1, replica_groups=mesh['member'=8,'region'=4] {'member'}, dimensions={0}, use_global_device_ids=true | all-gather | bytes 1152 | tf_op jit(solution)/shard_map/all_gather | solution.py:70
  133.9 8.9 %all-gather.1 = f32[8,2,16]{2,1,0:T(2,128)S(1)} all-gather(f32[1,2,16]{2,1,0:T(2,128)S(1)} %bitcast.94), channel_id=1, replica_groups=mesh['member'=8,'region'=4] {'member'}, dimensions={0}, use_global_device_ids=true | all-gather | bytes 1152 | tf_op jit(solution)/shard_map/all_gather | solution.py:70
  145.2 1.7 gather_fusion.2
  146.9 3.5 %all-to-all-start.3 = ((bf16[8,8,4096]{2,1,0:T(8,128)(2,1)}), bf16[8,8,4096]{2,1,0:T(8,128)(2,1)S(1)}, u32[]{:S(2)}, u32[]{:S(2)}) async-start(bf16[8,8,4096]{2,1,0:T(8,128)(2,1)} %bitcast.10), calls=%async_computation.3 | async-start | bytes 1048576 | tf_op jit(solution)/shard_map/all_to_all | solution.py:91
  150.4 16.3 %reduce-scatter.3.cloned.1.call-done = f32[16,512]{1,0:T(8,128)} async-done(((f32[16,4096]{1,0:T(8,128)}), f32[16,512]{1,0:T(8,128)}) %reduce-scatter.3.cloned.1.call-update) | async-done | bytes 32784 | tf_op jit(solution)/shard_map/reduce_scatter | solution.py:80
  167.5 36.7 %reduce-scatter.5.cloned.1.call-done = f32[16,512]{1,0:T(8,128)} async-done(((f32[16,4096]{1,0:T(8,128)}), f32[16,512]{1,0:T(8,128)}) %reduce-scatter.5.cloned.1.call-update) | async-done | bytes 32784 | tf_op jit(solution)/shard_map/reduce_scatter | solution.py:80
  205.7 2.1 gather_fusion.3
  (94 shorter events, 29.9 us)
Async XLA Ops:
  7.2 51.4 %copy-start = (f32[2,32,16]{1,2,0:T(8,128)S(1)}, f32[2,32,16]{1,2,0:T(8,128)}, u32[]{:S(2)}) copy-start(f32[2,32,16]{1,2,0:T(8,128)} %param.14) | copy-start | bytes 12292
  7.2 51.6 %copy-start.1 = (f32[32,16]{0,1:T(8,128)S(1)}, f32[32,16]{0,1:T(8,128)}, u32[]{:S(2)}) copy-start(f32[32,16]{0,1:T(8,128)} %param.15) | copy-start | bytes 6148
  7.2 51.7 %copy-start.3 = (s32[16,6]{0,1:T(8,128)S(1)}, s32[16,6]{0,1:T(8,128)}, u32[]{:S(2)}) copy-start(s32[16,6]{0,1:T(8,128)} %param.18) | copy-start | bytes 1156
  7.2 51.7 %copy-start.2 = (f32[16,6]{0,1:T(8,128)S(1)}, f32[16,6]{0,1:T(8,128)}, u32[]{:S(2)}) copy-start(f32[16,6]{0,1:T(8,128)} %param.19) | copy-start | bytes 1156
  8.7 28.7 %collective-permute-start = (f32[2,1]{1,0:T(2,128)S(1)}, f32[2,1]{1,0:T(2,128)S(1)}, u32[]{:S(2)}, u32[]{:S(2)}) collective-permute-start(f32[2,1]{1,0:T(2,128)S(1)} %get-tuple-element.16), channel_id=1, source_target_pairs={{0,1},{1,2},{2,3},{4,5},{5,6},{6,7},{8,9},{9,10},{10,11},{12,13},{... | collective-permute-start | bytes 32 | tf_op jit(solution)/shard_map/ppermute | solution.py:17
  13.6 23.8 %collective-permute-start.1 = (f32[2,1]{1,0:T(2,128)S(1)}, f32[2,1]{1,0:T(2,128)S(1)}, u32[]{:S(2)}, u32[]{:S(2)}) collective-permute-start(f32[2,1]{1,0:T(2,128)S(1)} %get-tuple-element.17), channel_id=1, source_target_pairs={{1,0},{2,1},{3,2},{5,4},{6,5},{7,6},{9,8},{10,9},{11,10},{13,12},{... | collective-permute-start | bytes 32 | tf_op jit(solution)/shard_map/ppermute | solution.py:18
  22.8 21.7 %all-to-all-start = ((s32[8,1,8]{2,1,0:T(1,128)}), s32[8,1,8]{2,1,0:T(1,128)S(1)}, u32[]{:S(2)}, u32[]{:S(2)}) async-start(s32[8,1,8]{2,1,0:T(1,128)} %bitcast.3), calls=%async_computation | async-start | bytes 8192 | tf_op jit(solution)/shard_map/all_to_all | solution.py:88
  38.6 10.1 %collective-permute-start.2 = (f32[2,1]{1,0:T(2,128)S(1)}, f32[2,1]{1,0:T(2,128)S(1)}, u32[]{:S(2)}, u32[]{:S(2)}) collective-permute-start(f32[2,1]{1,0:T(2,128)S(1)} %get-tuple-element.14), channel_id=1, source_target_pairs={{0,1},{1,2},{2,3},{4,5},{5,6},{6,7},{8,9},{9,10},{10,11},{12,13},{... | collective-permute-start | bytes 32 | tf_op jit(solution)/shard_map/ppermute | solution.py:17
  43.2 5.5 %collective-permute-start.3 = (f32[2,1]{1,0:T(2,128)S(1)}, f32[2,1]{1,0:T(2,128)S(1)}, u32[]{:S(2)}, u32[]{:S(2)}) collective-permute-start(f32[2,1]{1,0:T(2,128)S(1)} %get-tuple-element.15), channel_id=1, source_target_pairs={{1,0},{2,1},{3,2},{5,4},{6,5},{7,6},{9,8},{10,9},{11,10},{13,12},{... | collective-permute-start | bytes 32 | tf_op jit(solution)/shard_map/ppermute | solution.py:18
  44.5 8.8 %all-to-all-start.2 = ((s32[8,1,8]{2,1,0:T(1,128)}), s32[8,1,8]{2,1,0:T(1,128)S(1)}, u32[]{:S(2)}, u32[]{:S(2)}) async-start(s32[8,1,8]{2,1,0:T(1,128)} %bitcast.9), calls=%async_computation.2 | async-start | bytes 8192 | tf_op jit(solution)/shard_map/all_to_all | solution.py:88
  55.0 23.7 %all-to-all-start.1 = ((bf16[8,8,4096]{2,1,0:T(8,128)(2,1)}), bf16[8,8,4096]{2,1,0:T(8,128)(2,1)S(1)}, u32[]{:S(2)}, u32[]{:S(2)}) async-start(bf16[8,8,4096]{2,1,0:T(8,128)(2,1)} %bitcast.4), calls=%async_computation.1 | async-start | bytes 1048576 | tf_op jit(solution)/shard_map/all_to_all | solution.py:91
  58.5 108.1 %reduce-scatter.3.cloned.1.call-start = ((), (), s32[]{:S(2)}) async-start(), calls=%async_computation.6 | async-start | bytes 294912 | tf_op jit(solution)/shard_map/reduce_scatter | solution.py:80
  80.7 6.0 %collective-permute-start.4 = (f32[2,1]{1,0:T(2,128)S(1)}, f32[2,1]{1,0:T(2,128)S(1)}, u32[]{:S(2)}, u32[]{:S(2)}) collective-permute-start(f32[2,1]{1,0:T(2,128)S(1)} %get-tuple-element.12), channel_id=1, source_target_pairs={{0,1},{1,2},{2,3},{4,5},{5,6},{6,7},{8,9},{9,10},{10,11},{12,13},{... | collective-permute-start | bytes 32 | tf_op jit(solution)/shard_map/ppermute | solution.py:17
  85.2 5.5 %collective-permute-start.5 = (f32[2,1]{1,0:T(2,128)S(1)}, f32[2,1]{1,0:T(2,128)S(1)}, u32[]{:S(2)}, u32[]{:S(2)}) collective-permute-start(f32[2,1]{1,0:T(2,128)S(1)} %get-tuple-element.13), channel_id=1, source_target_pairs={{1,0},{2,1},{3,2},{5,4},{6,5},{7,6},{9,8},{10,9},{11,10},{13,12},{... | collective-permute-start | bytes 32 | tf_op jit(solution)/shard_map/ppermute | solution.py:18
  91.9 4.8 %collective-permute-start.6 = (f32[2,1]{1,0:T(2,128)S(1)}, f32[2,1]{1,0:T(2,128)S(1)}, u32[]{:S(2)}, u32[]{:S(2)}) collective-permute-start(f32[2,1]{1,0:T(2,128)S(1)} %get-tuple-element.10), channel_id=1, source_target_pairs={{0,1},{1,2},{2,3},{4,5},{5,6},{6,7},{8,9},{9,10},{10,11},{12,13},{... | collective-permute-start | bytes 32 | tf_op jit(solution)/shard_map/ppermute | solution.py:17
  95.4 5.5 %collective-permute-start.7 = (f32[2,1]{1,0:T(2,128)S(1)}, f32[2,1]{1,0:T(2,128)S(1)}, u32[]{:S(2)}, u32[]{:S(2)}) collective-permute-start(f32[2,1]{1,0:T(2,128)S(1)} %get-tuple-element.11), channel_id=1, source_target_pairs={{1,0},{2,1},{3,2},{5,4},{6,5},{7,6},{9,8},{10,9},{11,10},{13,12},{... | collective-permute-start | bytes 32 | tf_op jit(solution)/shard_map/ppermute | solution.py:18
  133.7 70.5 %reduce-scatter.5.cloned.1.call-start = ((), (), s32[]{:S(2)}) async-start(), calls=%async_computation.7 | async-start | bytes 294912 | tf_op jit(solution)/shard_map/reduce_scatter | solution.py:80
  146.9 58.8 %all-to-all-start.3 = ((bf16[8,8,4096]{2,1,0:T(8,128)(2,1)}), bf16[8,8,4096]{2,1,0:T(8,128)(2,1)S(1)}, u32[]{:S(2)}, u32[]{:S(2)}) async-start(bf16[8,8,4096]{2,1,0:T(8,128)(2,1)} %bitcast.10), calls=%async_computation.3 | async-start | bytes 1048576 | tf_op jit(solution)/shard_map/all_to_all | solution.py:91
Sparse Core Ops, SparseCore 0:
  133.8 32.8 reduce-scatter.2
  170.6 33.5 reduce-scatter.4
where the time goes:
time: 216 us; the launch traced here: 215 us
  local copies, waits for them, and re-layouts  65.8 us (30%)
  waiting for transfers between devices  64.3 us (30%)
  starting transfers between devices  37.8 us (17%)
  blocking collectives  18.1 us (8%)
  between operations  14.4 us (7%)
  other arithmetic  13.8 us (6%)
    reduce_scatter x2, waiting for transfers between devices, body(): lax.psum_scatter(weighted, 'member', scatter_dimension=1, tiled=True)  52.9 us
    convert_element_type x2, local copies, waits for them, and re-layouts, body(): prior_ensemble = (moved + model_perturbation[update_ordinal].reshape(part...  21.3 us
    all_gather x2, blocking collectives, body(): all_scores = lax.all_gather(loglik, 'member', axis=0, tiled=True)  18.1 us
    gather x2, local copies, waits for them, and re-layouts, body(): modelled_readings = prior_ensemble[:, measured_position].astype(jnp.float32)  18 us
    ppermute x4, starting transfers between devices, extended(): before = lax.ppermute(last, axis, up)  17.5 us
    scatter x2, local copies, waits for them, and re-layouts, body(): jnp.full((members, capacity), -1, jnp.int32).at[source, ranks].set(codes)  10.8 us
    ppermute x4, waiting for transfers between devices, extended(): after = lax.ppermute(initial, axis, down)  8.13 us
    all_to_all x2, starting transfers between devices, body(): lax.all_to_all(wanted, 'member', split_axis=0, concat_axis=0, tiled=True)  7.93 us
  transfers between devices with their start and end apart: 14, of which 5 were waited for; matrix products, arithmetic and copies ran while one was open for 22% of the time, Pallas kernels for 0%

commit v1 on v0

--- a/solution.py
+++ b/solution.py
@@ -67,7 +67,20 @@
         misses = obs_values[update_ordinal] - modelled_readings
         misfit = 0.5 * jnp.sum(obs_prec * misses * misses, axis=-1)
         loglik = jnp.dot(misfit, loc_matrix.T, precision=lax.Precision.HIGHEST)
-        all_scores = lax.all_gather(loglik, "member", axis=0, tiled=True)
+
+        def push_ticks(mine_x, bus_axis, along_dim):
+            extent = jax.lax.axis_size(bus_axis)
+            all_rows = [None] * extent
+            log = [(d, (d + 1) % extent) for d in range(extent)]
+            all_rows[extent - 1] = mine_x
+            for ii in range(extent - 2, -1, -1):
+                all_rows[ii] = jax.lax.ppermute(all_rows[ii + 1], axis_name=bus_axis, perm=log)
+            mixed_arr = jnp.concatenate(all_rows, axis=along_dim)
+            frame_out = jax.lax.axis_index(bus_axis)
+            met_up = (frame_out + 1) * mine_x.shape[along_dim]
+            return jnp.roll(mixed_arr, met_up, axis=along_dim)
+
+        all_scores = push_ticks(loglik, "member", 0)
         lowest = jnp.min(all_scores, axis=0)
         totals = jnp.sum(jnp.exp(lowest - all_scores), axis=0)
         unscaled = jnp.exp(lowest - loglik)

time: 216 us -> 241 us (1.12)
  waiting for transfers between devices: 64.3 us -> 103 us
  blocking collectives: 18.1 us -> 0 us
  starting transfers between devices: 37.8 us -> 41.9 us
    ppermute x0 -> x14, waiting for transfers between devices: none -> 26.6 us  [push_ticks(): jax.lax.ppermute(all_rows[ii + 1], axis_name=bus_axis, perm=log)]
    all_gather x2 -> x0, blocking collectives: 18.1 us -> none  [body(): all_scores = lax.all_gather(loglik, 'member', axis=0, tiled=True)]
    reduce_scatter x2, waiting for transfers between devices: 52.9 us -> 65.4 us  [body(): lax.psum_scatter(weighted, 'member', scatter_dimension=1, tiled=True)]
    ppermute x0 -> x14, starting transfers between devices: none -> 4.09 us  [push_ticks(): jax.lax.ppermute(all_rows[ii + 1], axis_name=bus_axis, perm=log)]
  transfers between devices with their start and end apart: 14 -> 28, of which waited for: 5 -> 15; matrix products, arithmetic and copies ran while one was open for 22% -> 21% of each run, Pallas kernels for 0% -> 0%
where the time goes in v1:
time: 241 us; the launch traced here: 240 us
  waiting for transfers between devices  103 us (43%)
  local copies, waits for them, and re-layouts  65.9 us (27%)
  starting transfers between devices  41.9 us (17%)
  between operations  14.4 us (6%)
  other arithmetic  13.8 us (6%)
    reduce_scatter x2, waiting for transfers between devices, body(): lax.psum_scatter(weighted, 'member', scatter_dimension=1, tiled=True)  65.4 us
    ppermute x14, waiting for transfers between devices, push_ticks(): jax.lax.ppermute(all_rows[ii + 1], axis_name=bus_axis, perm=log)  26.6 us
    convert_element_type x2, local copies, waits for them, and re-layouts, body(): prior_ensemble = (moved + model_perturbation[update_ordinal].reshape(part...  21.3 us
    gather x2, local copies, waits for them, and re-layouts, body(): modelled_readings = prior_ensemble[:, measured_position].astype(jnp.float32)  18 us
    ppermute x4, starting transfers between devices, extended(): before = lax.ppermute(last, axis, up)  17.5 us
    scatter x2, local copies, waits for them, and re-layouts, body(): jnp.full((members, capacity), -1, jnp.int32).at[source, ranks].set(codes)  10.8 us
    ppermute x4, waiting for transfers between devices, extended(): after = lax.ppermute(initial, axis, down)  8.13 us
    all_to_all x2, starting transfers between devices, body(): lax.all_to_all(wanted, 'member', split_axis=0, concat_axis=0, tiled=True)  7.93 us
  transfers between devices with their start and end apart: 28, of which 15 were waited for; matrix products, arithmetic and copies ran while one was open for 21% of the time, Pallas kernels for 0%

profile of v1, /device:TPU:0, one launch (start us, length us, event | category | flops | bytes accessed | tf_op | source)
XLA Modules:
  0.0 239.8 jit_solution(5055049928774001116)
XLA Ops:
  8.7 4.9 %collective-permute-start = (f32[2,1]{1,0:T(2,128)S(1)}, f32[2,1]{1,0:T(2,128)S(1)}, u32[]{:S(2)}, u32[]{:S(2)}) collective-permute-start(f32[2,1]{1,0:T(2,128)S(1)} %get-tuple-element.17), channel_id=1, source_target_pairs={{0,1},{1,2},{2,3},{4,5},{5,6},{6,7},{8,9},{9,10},{10,11},{12,13},{... | collective-permute-start | bytes 32 | tf_op jit(solution)/shard_map/ppermute | solution.py:17
  17.4 5.4 %scatter_fusion = s32[8,8]{1,0:T(8,128)} fusion(s32[8,8]{1,0:T(8,128)} %broadcast.130.clone.1, s32[32]{0:T(128)S(1)} %get-tuple-element.9, s32[32]{0:T(128)S(1)} %fusion.41), kind=kCustom, calls=%fused_computation.6 | custom fusion | bytes 640 | tf_op jit(solution)/shard_map/scatter | solution.py:98
  22.8 3.7 %all-to-all-start = ((s32[8,1,8]{2,1,0:T(1,128)}), s32[8,1,8]{2,1,0:T(1,128)S(1)}, u32[]{:S(2)}, u32[]{:S(2)}) async-start(s32[8,1,8]{2,1,0:T(1,128)} %bitcast.3), calls=%async_computation | async-start | bytes 8192 | tf_op jit(solution)/shard_map/all_to_all | solution.py:101
  32.0 5.4 %scatter_fusion.1 = s32[8,8]{1,0:T(8,128)} fusion(s32[8,8]{1,0:T(8,128)} %broadcast.130.clone, s32[32]{0:T(128)S(1)} %get-tuple-element.7, s32[32]{0:T(128)S(1)} %fusion.40), kind=kCustom, calls=%fused_computation.7 | custom fusion | bytes 640 | tf_op jit(solution)/shard_map/scatter | solution.py:98
  38.6 4.5 %collective-permute-start.2 = (f32[2,1]{1,0:T(2,128)S(1)}, f32[2,1]{1,0:T(2,128)S(1)}, u32[]{:S(2)}, u32[]{:S(2)}) collective-permute-start(f32[2,1]{1,0:T(2,128)S(1)} %get-tuple-element.15), channel_id=1, source_target_pairs={{0,1},{1,2},{2,3},{4,5},{5,6},{6,7},{8,9},{9,10},{10,11},{12,13},{... | collective-permute-start | bytes 32 | tf_op jit(solution)/shard_map/ppermute | solution.py:17
  44.5 4.2 %all-to-all-start.2 = ((s32[8,1,8]{2,1,0:T(1,128)}), s32[8,1,8]{2,1,0:T(1,128)S(1)}, u32[]{:S(2)}, u32[]{:S(2)}) async-start(s32[8,1,8]{2,1,0:T(1,128)} %bitcast.9), calls=%async_computation.2 | async-start | bytes 8192 | tf_op jit(solution)/shard_map/all_to_all | solution.py:101
  55.0 3.5 %all-to-all-start.1 = ((bf16[8,8,4096]{2,1,0:T(8,128)(2,1)}), bf16[8,8,4096]{2,1,0:T(8,128)(2,1)S(1)}, u32[]{:S(2)}, u32[]{:S(2)}) async-start(bf16[8,8,4096]{2,1,0:T(8,128)(2,1)} %bitcast.4), calls=%async_computation.1 | async-start | bytes 1048576 | tf_op jit(solution)/shard_map/all_to_all | solution.py:104
  58.9 10.7 %copy.139 = bf16[2,65536]{0,1:T(8,128)(2,1)} copy(bf16[2,65536]{1,0:T(2,128)(2,1)S(1)} %fusion.18) | data formatting | bytes 524288 | tf_op jit(solution)/shard_map/convert_element_type | solution.py:65
  69.6 9.0 %gather_fusion.4 = bf16[512,2]{1,0:T(8,128)(2,1)S(1)} fusion(bf16[2,65536]{0,1:T(8,128)(2,1)} %copy.139, s32[1024]{0:T(1024)S(1)} %pad_clamp_fusion), kind=kCustom, calls=%fused_computation.4 | custom fusion | bytes 6144 | tf_op jit(solution)/shard_map/gather | solution.py:66
  80.7 4.6 %collective-permute-start.4 = (f32[2,1]{1,0:T(2,128)S(1)}, f32[2,1]{1,0:T(2,128)S(1)}, u32[]{:S(2)}, u32[]{:S(2)}) collective-permute-start(f32[2,1]{1,0:T(2,128)S(1)} %get-tuple-element.13), channel_id=1, source_target_pairs={{0,1},{1,2},{2,3},{4,5},{5,6},{6,7},{8,9},{9,10},{10,11},{12,13},{... | collective-permute-start | bytes 32 | tf_op jit(solution)/shard_map/ppermute | solution.py:17
  86.7 4.0 %collective-permute-done.5 = f32[2,1]{1,0:T(2,128)S(1)} collective-permute-done((f32[2,1]{1,0:T(2,128)S(1)}, f32[2,1]{1,0:T(2,128)S(1)}, u32[]{:S(2)}, u32[]{:S(2)}) %collective-permute-start.5) | collective-permute-done | bytes 40 | tf_op jit(solution)/shard_map/ppermute | solution.py:18
  91.9 3.5 %collective-permute-start.6 = (f32[2,1]{1,0:T(2,128)S(1)}, f32[2,1]{1,0:T(2,128)S(1)}, u32[]{:S(2)}, u32[]{:S(2)}) collective-permute-start(f32[2,1]{1,0:T(2,128)S(1)} %get-tuple-element.11), channel_id=1, source_target_pairs={{0,1},{1,2},{2,3},{4,5},{5,6},{6,7},{8,9},{9,10},{10,11},{12,13},{... | collective-permute-start | bytes 32 | tf_op jit(solution)/shard_map/ppermute | solution.py:17
  96.7 4.2 %collective-permute-done.7 = f32[2,1]{1,0:T(2,128)S(1)} collective-permute-done((f32[2,1]{1,0:T(2,128)S(1)}, f32[2,1]{1,0:T(2,128)S(1)}, u32[]{:S(2)}, u32[]{:S(2)}) %collective-permute-start.7) | collective-permute-done | bytes 40 | tf_op jit(solution)/shard_map/ppermute | solution.py:18
  102.0 10.7 %copy.141 = bf16[2,65536]{0,1:T(8,128)(2,1)} copy(bf16[2,65536]{1,0:T(2,128)(2,1)S(1)} %fusion.19) | data formatting | bytes 524288 | tf_op jit(solution)/shard_map/convert_element_type | solution.py:65
  112.9 9.0 %gather_fusion.5 = bf16[512,2]{1,0:T(8,128)(2,1)S(1)} fusion(bf16[2,65536]{0,1:T(8,128)(2,1)} %copy.141, s32[1024]{0:T(1024)S(1)} %pad_clamp_fusion), kind=kCustom, calls=%fused_computation.5 | custom fusion | bytes 6144 | tf_op jit(solution)/shard_map/gather | solution.py:66
  126.3 3.5 %all-to-all-start.3 = ((bf16[8,8,4096]{2,1,0:T(8,128)(2,1)}), bf16[8,8,4096]{2,1,0:T(8,128)(2,1)S(1)}, u32[]{:S(2)}, u32[]{:S(2)}) async-start(bf16[8,8,4096]{2,1,0:T(8,128)(2,1)} %bitcast.10), calls=%async_computation.3 | async-start | bytes 1048576 | tf_op jit(solution)/shard_map/all_to_all | solution.py:104
  131.9 7.2 %collective-permute-done.9 = f32[2,16]{1,0:T(2,128)S(1)} collective-permute-done((f32[2,16]{1,0:T(2,128)S(1)}, f32[2,16]{1,0:T(2,128)S(1)}, u32[]{:S(2)}, u32[]{:S(2)}) %collective-permute-start.9) | collective-permute-done | bytes 160 | tf_op jit(solution)/shard_map/ppermute | solution.py:77
  139.1 3.9 %collective-permute-done.10 = f32[2,16]{1,0:T(2,128)S(1)} collective-permute-done((f32[2,16]{1,0:T(2,128)S(1)}, f32[2,16]{1,0:T(2,128)S(1)}, u32[]{:S(2)}, u32[]{:S(2)}) %collective-permute-start.10) | collective-permute-done | bytes 160 | tf_op jit(solution)/shard_map/ppermute | solution.py:77
  143.0 3.8 %collective-permute-done.11 = f32[2,16]{1,0:T(2,128)S(1)} collective-permute-done((f32[2,16]{1,0:T(2,128)S(1)}, f32[2,16]{1,0:T(2,128)S(1)}, u32[]{:S(2)}, u32[]{:S(2)}) %collective-permute-start.11) | collective-permute-done | bytes 160 | tf_op jit(solution)/shard_map/ppermute | solution.py:77
  146.9 3.8 %collective-permute-done.12 = f32[2,16]{1,0:T(2,128)S(1)} collective-permute-done((f32[2,16]{1,0:T(2,128)S(1)}, f32[2,16]{1,0:T(2,128)S(1)}, u32[]{:S(2)}, u32[]{:S(2)}) %collective-permute-start.12) | collective-permute-done | bytes 160 | tf_op jit(solution)/shard_map/ppermute | solution.py:77
  150.8 3.8 %collective-permute-done.13 = f32[2,16]{1,0:T(2,128)S(1)} collective-permute-done((f32[2,16]{1,0:T(2,128)S(1)}, f32[2,16]{1,0:T(2,128)S(1)}, u32[]{:S(2)}, u32[]{:S(2)}) %collective-permute-start.13) | collective-permute-done | bytes 160 | tf_op jit(solution)/shard_map/ppermute | solution.py:77
  154.7 3.8 %collective-permute-done.14 = f32[2,16]{1,0:T(2,128)S(1)} collective-permute-done((f32[2,16]{1,0:T(2,128)S(1)}, f32[2,16]{1,0:T(2,128)S(1)}, u32[]{:S(2)}, u32[]{:S(2)}) %collective-permute-start.14) | collective-permute-done | bytes 160 | tf_op jit(solution)/shard_map/ppermute | solution.py:77
  163.2 28.7 %reduce-scatter.3.cloned.1.call-done = f32[16,512]{1,0:T(8,128)} async-done(((f32[16,4096]{1,0:T(8,128)}), f32[16,512]{1,0:T(8,128)}) %reduce-scatter.3.cloned.1.call-update) | async-done | bytes 32784 | tf_op jit(solution)/shard_map/reduce_scatter | solution.py:93
  192.7 36.7 %reduce-scatter.5.cloned.1.call-done = f32[16,512]{1,0:T(8,128)} async-done(((f32[16,4096]{1,0:T(8,128)}), f32[16,512]{1,0:T(8,128)}) %reduce-scatter.5.cloned.1.call-update) | async-done | bytes 32784 | tf_op jit(solution)/shard_map/reduce_scatter | solution.py:93
  (122 shorter events, 43.1 us)
Async XLA Ops:
  8.7 28.7 %collective-permute-start = (f32[2,1]{1,0:T(2,128)S(1)}, f32[2,1]{1,0:T(2,128)S(1)}, u32[]{:S(2)}, u32[]{:S(2)}) collective-permute-start(f32[2,1]{1,0:T(2,128)S(1)} %get-tuple-element.17), channel_id=1, source_target_pairs={{0,1},{1,2},{2,3},{4,5},{5,6},{6,7},{8,9},{9,10},{10,11},{12,13},{... | collective-permute-start | bytes 32 | tf_op jit(solution)/shard_map/ppermute | solution.py:17
  13.6 23.8 %collective-permute-start.1 = (f32[2,1]{1,0:T(2,128)S(1)}, f32[2,1]{1,0:T(2,128)S(1)}, u32[]{:S(2)}, u32[]{:S(2)}) collective-permute-start(f32[2,1]{1,0:T(2,128)S(1)} %get-tuple-element.18), channel_id=1, source_target_pairs={{1,0},{2,1},{3,2},{5,4},{6,5},{7,6},{9,8},{10,9},{11,10},{13,12},{... | collective-permute-start | bytes 32 | tf_op jit(solution)/shard_map/ppermute | solution.py:18
  22.8 21.7 %all-to-all-start = ((s32[8,1,8]{2,1,0:T(1,128)}), s32[8,1,8]{2,1,0:T(1,128)S(1)}, u32[]{:S(2)}, u32[]{:S(2)}) async-start(s32[8,1,8]{2,1,0:T(1,128)} %bitcast.3), calls=%async_computation | async-start | bytes 8192 | tf_op jit(solution)/shard_map/all_to_all | solution.py:101
  38.6 10.1 %collective-permute-start.2 = (f32[2,1]{1,0:T(2,128)S(1)}, f32[2,1]{1,0:T(2,128)S(1)}, u32[]{:S(2)}, u32[]{:S(2)}) collective-permute-start(f32[2,1]{1,0:T(2,128)S(1)} %get-tuple-element.15), channel_id=1, source_target_pairs={{0,1},{1,2},{2,3},{4,5},{5,6},{6,7},{8,9},{9,10},{10,11},{12,13},{... | collective-permute-start | bytes 32 | tf_op jit(solution)/shard_map/ppermute | solution.py:17
  43.2 5.5 %collective-permute-start.3 = (f32[2,1]{1,0:T(2,128)S(1)}, f32[2,1]{1,0:T(2,128)S(1)}, u32[]{:S(2)}, u32[]{:S(2)}) collective-permute-start(f32[2,1]{1,0:T(2,128)S(1)} %get-tuple-element.16), channel_id=1, source_target_pairs={{1,0},{2,1},{3,2},{5,4},{6,5},{7,6},{9,8},{10,9},{11,10},{13,12},{... | collective-permute-start | bytes 32 | tf_op jit(solution)/shard_map/ppermute | solution.py:18
  44.5 8.8 %all-to-all-start.2 = ((s32[8,1,8]{2,1,0:T(1,128)}), s32[8,1,8]{2,1,0:T(1,128)S(1)}, u32[]{:S(2)}, u32[]{:S(2)}) async-start(s32[8,1,8]{2,1,0:T(1,128)} %bitcast.9), calls=%async_computation.2 | async-start | bytes 8192 | tf_op jit(solution)/shard_map/all_to_all | solution.py:101
  55.0 23.6 %all-to-all-start.1 = ((bf16[8,8,4096]{2,1,0:T(8,128)(2,1)}), bf16[8,8,4096]{2,1,0:T(8,128)(2,1)S(1)}, u32[]{:S(2)}, u32[]{:S(2)}) async-start(bf16[8,8,4096]{2,1,0:T(8,128)(2,1)} %bitcast.4), calls=%async_computation.1 | async-start | bytes 1048576 | tf_op jit(solution)/shard_map/all_to_all | solution.py:104
  80.7 6.1 %collective-permute-start.4 = (f32[2,1]{1,0:T(2,128)S(1)}, f32[2,1]{1,0:T(2,128)S(1)}, u32[]{:S(2)}, u32[]{:S(2)}) collective-permute-start(f32[2,1]{1,0:T(2,128)S(1)} %get-tuple-element.13), channel_id=1, source_target_pairs={{0,1},{1,2},{2,3},{4,5},{5,6},{6,7},{8,9},{9,10},{10,11},{12,13},{... | collective-permute-start | bytes 32 | tf_op jit(solution)/shard_map/ppermute | solution.py:17
  85.2 5.5 %collective-permute-start.5 = (f32[2,1]{1,0:T(2,128)S(1)}, f32[2,1]{1,0:T(2,128)S(1)}, u32[]{:S(2)}, u32[]{:S(2)}) collective-permute-start(f32[2,1]{1,0:T(2,128)S(1)} %get-tuple-element.14), channel_id=1, source_target_pairs={{1,0},{2,1},{3,2},{5,4},{6,5},{7,6},{9,8},{10,9},{11,10},{13,12},{... | collective-permute-start | bytes 32 | tf_op jit(solution)/shard_map/ppermute | solution.py:18
  91.9 4.8 %collective-permute-start.6 = (f32[2,1]{1,0:T(2,128)S(1)}, f32[2,1]{1,0:T(2,128)S(1)}, u32[]{:S(2)}, u32[]{:S(2)}) collective-permute-start(f32[2,1]{1,0:T(2,128)S(1)} %get-tuple-element.11), channel_id=1, source_target_pairs={{0,1},{1,2},{2,3},{4,5},{5,6},{6,7},{8,9},{9,10},{10,11},{12,13},{... | collective-permute-start | bytes 32 | tf_op jit(solution)/shard_map/ppermute | solution.py:17
  95.4 5.5 %collective-permute-start.7 = (f32[2,1]{1,0:T(2,128)S(1)}, f32[2,1]{1,0:T(2,128)S(1)}, u32[]{:S(2)}, u32[]{:S(2)}) collective-permute-start(f32[2,1]{1,0:T(2,128)S(1)} %get-tuple-element.12), channel_id=1, source_target_pairs={{1,0},{2,1},{3,2},{5,4},{6,5},{7,6},{9,8},{10,9},{11,10},{13,12},{... | collective-permute-start | bytes 32 | tf_op jit(solution)/shard_map/ppermute | solution.py:18
  122.4 7.4 %collective-permute-start.8 = (f32[2,16]{1,0:T(2,128)S(1)}, f32[2,16]{1,0:T(2,128)S(1)}, u32[]{:S(2)}, u32[]{:S(2)}) collective-permute-start(f32[2,16]{1,0:T(2,128)S(1)} %fusion.26), channel_id=1, source_target_pairs={{0,4},{4,8},{8,12},{12,16},{16,20},{20,24},{24,28},{28,0},{1,5},{5... | collective-permute-start | bytes 392 | tf_op jit(solution)/shard_map/ppermute | solution.py:77
  122.6 7.6 %collective-permute-start.15 = (f32[2,16]{1,0:T(2,128)S(1)}, f32[2,16]{1,0:T(2,128)S(1)}, u32[]{:S(2)}, u32[]{:S(2)}) collective-permute-start(f32[2,16]{1,0:T(2,128)S(1)} %fusion.24), channel_id=1, source_target_pairs={{0,4},{4,8},{8,12},{12,16},{16,20},{20,24},{24,28},{28,0},{1,5},{5... | collective-permute-start | bytes 392 | tf_op jit(solution)/shard_map/ppermute | solution.py:77
  126.3 104.6 %all-to-all-start.3 = ((bf16[8,8,4096]{2,1,0:T(8,128)(2,1)}), bf16[8,8,4096]{2,1,0:T(8,128)(2,1)S(1)}, u32[]{:S(2)}, u32[]{:S(2)}) async-start(bf16[8,8,4096]{2,1,0:T(8,128)(2,1)} %bitcast.10), calls=%async_computation.3 | async-start | bytes 1048576 | tf_op jit(solution)/shard_map/all_to_all | solution.py:104
  129.8 62.1 %reduce-scatter.3.cloned.1.call-start = ((), (), s32[]{:S(2)}) async-start(), calls=%async_computation.6 | async-start | bytes 294912 | tf_op jit(solution)/shard_map/reduce_scatter | solution.py:93
  129.9 9.2 %collective-permute-start.9 = (f32[2,16]{1,0:T(2,128)S(1)}, f32[2,16]{1,0:T(2,128)S(1)}, u32[]{:S(2)}, u32[]{:S(2)}) collective-permute-start(f32[2,16]{1,0:T(2,128)S(1)} %collective-permute-done.8), channel_id=1, source_target_pairs={{0,4},{4,8},{8,12},{12,16},{16,20},{20,24},{24,28},{28,0},{1,5},{5... | collective-permute-start | bytes 392 | tf_op jit(solution)/shard_map/ppermute | solution.py:77
  130.3 8.8 %collective-permute-start.16 = (f32[2,16]{1,0:T(2,128)S(1)}, f32[2,16]{1,0:T(2,128)S(1)}, u32[]{:S(2)}, u32[]{:S(2)}) collective-permute-start(f32[2,16]{1,0:T(2,128)S(1)} %collective-permute-done.15), channel_id=1, source_target_pairs={{0,4},{4,8},{8,12},{12,16},{16,20},{20,24},{24,28},{28,0},{1,5},{5... | collective-permute-start | bytes 392 | tf_op jit(solution)/shard_map/ppermute | solution.py:77
  139.1 3.9 %collective-permute-start.10 = (f32[2,16]{1,0:T(2,128)S(1)}, f32[2,16]{1,0:T(2,128)S(1)}, u32[]{:S(2)}, u32[]{:S(2)}) collective-permute-start(f32[2,16]{1,0:T(2,128)S(1)} %collective-permute-done.9), channel_id=1, source_target_pairs={{0,4},{4,8},{8,12},{12,16},{16,20},{20,24},{24,28},{28,0},{1,5},{5... | collective-permute-start | bytes 392 | tf_op jit(solution)/shard_map/ppermute | solution.py:77
  139.1 3.9 %collective-permute-start.17 = (f32[2,16]{1,0:T(2,128)S(1)}, f32[2,16]{1,0:T(2,128)S(1)}, u32[]{:S(2)}, u32[]{:S(2)}) collective-permute-start(f32[2,16]{1,0:T(2,128)S(1)} %collective-permute-done.16), channel_id=1, source_target_pairs={{0,4},{4,8},{8,12},{12,16},{16,20},{20,24},{24,28},{28,0},{1,5},{5... | collective-permute-start | bytes 392 | tf_op jit(solution)/shard_map/ppermute | solution.py:77
  146.8 3.9 %collective-permute-start.12 = (f32[2,16]{1,0:T(2,128)S(1)}, f32[2,16]{1,0:T(2,128)S(1)}, u32[]{:S(2)}, u32[]{:S(2)}) collective-permute-start(f32[2,16]{1,0:T(2,128)S(1)} %collective-permute-done.11), channel_id=1, source_target_pairs={{0,4},{4,8},{8,12},{12,16},{16,20},{20,24},{24,28},{28,0},{1,5},{5... | collective-permute-start | bytes 392 | tf_op jit(solution)/shard_map/ppermute | solution.py:77
  146.9 3.9 %collective-permute-start.19 = (f32[2,16]{1,0:T(2,128)S(1)}, f32[2,16]{1,0:T(2,128)S(1)}, u32[]{:S(2)}, u32[]{:S(2)}) collective-permute-start(f32[2,16]{1,0:T(2,128)S(1)} %collective-permute-done.18), channel_id=1, source_target_pairs={{0,4},{4,8},{8,12},{12,16},{16,20},{20,24},{24,28},{28,0},{1,5},{5... | collective-permute-start | bytes 392 | tf_op jit(solution)/shard_map/ppermute | solution.py:77
  150.7 3.9 %collective-permute-start.13 = (f32[2,16]{1,0:T(2,128)S(1)}, f32[2,16]{1,0:T(2,128)S(1)}, u32[]{:S(2)}, u32[]{:S(2)}) collective-permute-start(f32[2,16]{1,0:T(2,128)S(1)} %collective-permute-done.12), channel_id=1, source_target_pairs={{0,4},{4,8},{8,12},{12,16},{16,20},{20,24},{24,28},{28,0},{1,5},{5... | collective-permute-start | bytes 392 | tf_op jit(solution)/shard_map/ppermute | solution.py:77
  154.7 6.1 %collective-permute-start.21 = (f32[2,16]{1,0:T(2,128)S(1)}, f32[2,16]{1,0:T(2,128)S(1)}, u32[]{:S(2)}, u32[]{:S(2)}) collective-permute-start(f32[2,16]{1,0:T(2,128)S(1)} %collective-permute-done.20), channel_id=1, source_target_pairs={{0,4},{4,8},{8,12},{12,16},{16,20},{20,24},{24,28},{28,0},{1,5},{5... | collective-permute-start | bytes 392 | tf_op jit(solution)/shard_map/ppermute | solution.py:77
  160.8 68.6 %reduce-scatter.5.cloned.1.call-start = ((), (), s32[]{:S(2)}) async-start(), calls=%async_computation.7 | async-start | bytes 294912 | tf_op jit(solution)/shard_map/reduce_scatter | solution.py:93
  (8 other events, 221.7 us)
Sparse Core Ops, SparseCore 0:
  160.9 30.9 reduce-scatter.2
  195.8 33.5 reduce-scatter.4
